TPU v7x, 32 devices: a whole 2x2x4 slice. The times are simulated.
32 devices in a mesh: dp: 8 (over z, y), sub: 4 (over x, core).
Axes of the slice: x: 2, y: 2, z: 4, core: 2. Of those that a mesh axis runs over, the one named last changes fastest.
Arguments:
- vectors: bfloat16 [4096, 2048], P(('dp', 'sub')), may hold values from -6 to 6
- rotation: bfloat16 [2048, 2048], P(None, 'sub'), may hold values from -0.125 to 0.125
- codebook: bfloat16 [16, 4096, 128], P('sub'), may hold values from -6 to 6
- codes: int32 [4096, 16], P('dp', 'sub'), may hold values from 0 to 4095
Outputs:
- centroids: bfloat16 [16, 4096, 128], P('sub')
- distortion: float32 [4096, 16], P('dp', 'sub')
- cross: float32 [2048, 2048], P('dp', 'sub')
All inputs are finite; a program needn't handle non-finite values.
Results may differ from a plain program's by a relative error of at most 0.0047.
Values may be sent and summed in bfloat16 or wider, within the bound.
No kernel may reach another device: no remote copies, remote signals or barrier semaphores. Data moves between devices by JAX's collectives and lax.ppermute only.
A program may use at most 64 MiB of HBM per device.

v0:
```python
import jax
import jax.numpy as jnp
from jax import lax
from jax.sharding import PartitionSpec as P


def class_sums(values, labels, count):
    totals = jax.ops.segment_sum(values.astype(jnp.float32), labels, num_segments=count)
    members = jax.ops.segment_sum(jnp.ones(labels.shape, jnp.float32), labels, num_segments=count)
    return (totals, members)


def update_rule(totals, members, codewords):
    return ((totals + codewords.astype(jnp.float32)) / (members[..., None] + 1.0)).astype(
        jnp.bfloat16
    )


def per_device(vectors, rotation, codebook, codes):
    local_sub = codebook.shape[0]
    count = codebook.shape[1]
    sub_width = codebook.shape[2]
    rotated = jnp.dot(
        vectors,
        lax.all_gather(rotation, "sub", axis=1, tiled=True),
        preferred_element_type=jnp.float32,
    ).astype(jnp.bfloat16)
    grouped = lax.all_to_all(rotated, "sub", split_axis=1, concat_axis=0, tiled=True)
    group_rows = grouped.shape[0]
    values = grouped.reshape(group_rows, local_sub, sub_width).transpose(1, 0, 2)
    labels = codes.T
    totals, members = jax.vmap(class_sums, in_axes=(0, 0, None))(values, labels, count)
    totals, members = lax.psum((totals, members), "dp")
    centroid = update_rule(totals, members, codebook)
    rebuilt = jax.vmap(lambda table, index: jnp.take(table, index, axis=0))(centroid, labels)
    distance = jnp.sum((values.astype(jnp.float32) - rebuilt.astype(jnp.float32)) ** 2, axis=-1)
    rebuilt_flat = rebuilt.transpose(1, 0, 2).reshape(group_rows, local_sub * sub_width)
    gathered = lax.all_gather(vectors, "sub", axis=0, tiled=True)
    product = lax.dot_general(
        gathered, rebuilt_flat, (((0,), (0,)), ((), ())), preferred_element_type=jnp.float32
    )
    cross = lax.psum_scatter(product, "dp", scatter_dimension=0, tiled=True)
    return (centroid, distance.T, cross)


def solution(mesh):
    placed = (P(("dp", "sub"), None), P(None, "sub"), P("sub", None, None), P("dp", "sub"))
    return jax.shard_map(
        per_device,
        mesh=mesh,
        in_specs=placed,
        out_specs=(P("sub", None, None), P("dp", "sub"), P("dp", "sub")),
        check_vma=False,
    )
```

profile of v0, /device:TPU:0, one launch (start us, length us, event | category | flops | bytes accessed | tf_op | source)
XLA Modules:
  0.0 516.5 jit_solution(4173967310708549093)
XLA Ops:
  7.2 0.0 all-gather.3.cloned.1.call-start
  7.2 0.7 all-gather.3.cloned.1.call-update
  7.9 0.0 copy-start
  7.9 0.0 copy-start.1
  7.9 0.0 copy-start.2
  7.9 62.6 %all-gather.3.cloned.1.call-done = bf16[2048,2048]{1,0:T(8,128)(2,1)} async-done(((bf16[2048,512]{1,0:T(8,128)(2,1)}), bf16[2048,2048]{1,0:T(8,128)(2,1)}) %all-gather.3.cloned.1.call-update) | async-done | bytes 8388624 | tf_op jit(solution)/shard_map/all_gather | solution.py:25
  70.6 4.8 convolution_convert_fusion
  75.4 0.8 copy.33
  76.2 3.5 all-to-all-start
  79.7 0.0 all-reduce.3.cloned.1.call-start
  79.8 0.0 copy-done
  79.8 0.0 copy-done.1
  79.8 0.1 multiply_reduce_fusion.1
  79.9 0.0 copy-done.2
  79.9 0.1 and_reduce_fusion
  80.0 11.3 %scatter_custom_fusion.1 = f32[16384]{0:T(1024)S(1)} fusion(s32[2048]{0:T(1024)S(1)} %bitcast.51, f32[2048]{0:T(1024)S(1)} %broadcast.41, f32[]{:T(128)} %constant.6.clone.1), kind=kCustom, calls=%fused_computation.13 | custom fusion | flops 2048 | bytes 65540
  91.3 0.7 reshape.31
  91.9 0.0 all-to-all-done
  91.9 0.1 convert_bitcast_fusion
  92.1 0.4 reshape.32
  92.4 0.1 copy.20
  92.5 15.2 %scatter_custom_fusion = f32[16384,128]{1,0:T(8,128)} fusion(s32[2048]{0:T(1024)S(1)} %bitcast.52, f32[2048,128]{1,0:T(8,128)S(1)} %bitcast.47, f32[]{:T(128)} %constant.6.clone.1), kind=kCustom, calls=%fused_computation.4 | custom fusion | flops 262144 | bytes 8388612
  107.7 0.0 all-reduce.3.cloned.1.call-update
  107.7 0.0 all-gather.5.cloned.1.call-start
  107.7 0.7 all-gather.5.cloned.1.call-update
  108.4 0.2 reduce-scatter.2.cloned.1.call-start
  108.7 271.5 %all-reduce.3.cloned.1.call-done = (f32[4,4096,128]{2,1,0:T(8,128)}, f32[4,4096]{1,0:T(4,128)}) async-done(((f32[4,4096,128]{2,1,0:T(8,128)}, f32[4,4096]{1,0:T(4,128)}), (f32[4,4096,128]{2,1,0:T(8,128)}, f32[4,4096]{1,0:T(4,128)})) %all-reduce.3.cloned.1.call-update) | async-done | bytes 8454160 | tf_op jit(solution)/shard_map/psum | solution.py:33
  380.2 0.9 broadcast_add_fusion
  381.1 8.3 %divide_convert_fusion = bf16[4,4096,128]{2,1,0:T(8,128)(2,1)} fusion(f32[4,4096,128]{2,1,0:T(8,128)} %get-tuple-element.15, bf16[4,4096,128]{2,1,0:T(8,128)(2,1)} %param.6, f32[4,4096]{1,0:T(4,128)S(1)} %broadcast_add_fusion), kind=kLoop, calls=%fused_computation.3 | loop fusion | flops 8388608 | bytes 16842752 | tf_op jit(solution)/shard_map/convert_element_type | solution.py:14
  389.4 25.7 %gather_fusion = bf16[2048,128]{1,0:T(8,128)(2,1)S(1)} fusion(bf16[4,4096,128]{2,1,0:T(8,128)(2,1)} %divide_convert_fusion, s32[2048]{0:T(1024)S(1)} %bitcast.40), kind=kCustom, calls=%fused_computation | custom fusion | bytes 1064960 | tf_op jit(solution)/shard_map/vmap(jit(_take))/gather | solution.py:35
  415.1 0.2 copy.23
  415.3 0.1 bitcast_select_fusion
  415.4 0.0 all-gather.5.cloned.1.call-done
  415.4 4.8 convolution_bitcast_fusion
  420.2 0.0 reduce-scatter.2.cloned.1.call-update
  420.2 0.2 copy.21
  420.4 7.3 %multiply_reduce_fusion = f32[4,512]{0,1:T(8,128)S(1)} fusion(bf16[4,512,128]{2,1,0:T(8,128)(2,1)S(1)} %bitcast.44, pred[4,512]{0,1:T(8,128)(4,1)S(1)} %copy.21, f32[512,4,128]{2,1,0:T(4,128)S(1)} %reshape.32), kind=kLoop, calls=%fused_computation.9 | loop fusion | flops 1308672 | bytes 1583104 | tf_op jit(solution)/shard_map/reduce_sum | solution.py:36
  427.7 0.7 copy.24
  428.4 79.6 %reduce-scatter.2.cloned.1.call-done = f32[256,512]{0,1:T(8,128)} async-done(((f32[2048,512]{0,1:T(8,128)}), f32[256,512]{0,1:T(8,128)}) %reduce-scatter.2.cloned.1.call-update) | async-done | bytes 524304 | tf_op jit(solution)/shard_map/reduce_scatter | solution.py:42
  508.0 2.0 copy.25
  (8 shorter events, 0.1 us)
Async XLA Ops:
  7.2 63.4 %all-gather.3.cloned.1.call-start = ((), (), s32[]{:S(2)}) async-start(), calls=%async_computation.2 | async-start | bytes 10485760 | tf_op jit(solution)/shard_map/all_gather | solution.py:25
  7.9 71.9 %copy-start = (s32[512,4]{0,1:T(4,128)S(1)}, s32[512,4]{0,1:T(4,128)}, u32[]{:S(2)}) copy-start(s32[512,4]{0,1:T(4,128)} %param.7) | copy-start | bytes 24580
  7.9 71.9 %copy-start.1 = (s32[2]{0:T(128)S(1)}, s32[2]{0:T(128)}, u32[]{:S(2)}) copy-start(s32[2]{0:T(128)} %constant.23) | copy-start | bytes 28
  7.9 71.9 %copy-start.2 = (s32[2]{0:T(128)S(1)}, s32[2]{0:T(128)}, u32[]{:S(2)}) copy-start(s32[2]{0:T(128)} %constant.26) | copy-start | bytes 28
  76.2 15.7 %all-to-all-start = ((bf16[128,4,512]{2,0,1:T(8,128)(2,1)}), bf16[128,4,512]{2,0,1:T(8,128)(2,1)S(1)}, u32[]{:S(2)}, u32[]{:S(2)}) async-start(bf16[128,4,512]{2,0,1:T(8,128)(2,1)} %bitcast.39), calls=%async_computation | async-start | bytes 1048576 | tf_op jit(solution)/shard_map/all_to_all | solution.py:28
  79.7 300.5 %all-reduce.3.cloned.1.call-start = ((), (), s32[]{:S(2)}) async-start(), calls=%async_computation.5 | async-start | bytes 16908288 | tf_op jit(solution)/shard_map/psum | solution.py:33
  107.7 307.7 %all-gather.5.cloned.1.call-start = ((), (), s32[]{:S(2)}) async-start(), calls=%async_computation.3 | async-start | bytes 2621440 | tf_op jit(solution)/shard_map/all_gather | solution.py:38
  108.4 399.5 %reduce-scatter.2.cloned.1.call-start = ((), (), s32[]{:S(2)}) async-start(), calls=%async_computation.4 | async-start | bytes 4718592 | tf_op jit(solution)/shard_map/reduce_scatter | solution.py:42
Sparse Core Ops, SparseCore 0:
  9.5 60.9 all-gather.2
  107.8 272.3 all-reduce.2
  381.8 21.6 all-gather.4
  420.3 87.5 reduce-scatter.1
where the time goes:
time: 517 us
  waiting for transfers between devices  415 us (80%)
  other arithmetic  43.2 us (8%)
  local copies, waits for them, and re-layouts  30.9 us (6%)
  between operations  13.9 us (3%)
  matrix products  9.6 us (2%)
    psum x1, waiting for transfers between devices, per_device(): totals, members = lax.psum((totals, members), 'dp')  271 us
    reduce_scatter x1, waiting for transfers between devices, per_device(): cross = lax.psum_scatter(product, 'dp', scatter_dimension=0, tiled=True)  79.6 us
    all_gather x1, waiting for transfers between devices, per_device(): lax.all_gather(rotation, 'sub', axis=1, tiled=True)  62.6 us
    unnamed x6, other arithmetic  26.6 us
    gather x2, local copies, waits for them, and re-layouts, per_device(): jnp.take(table, index, axis=0)  26 us
  transfers between devices with their start and end apart: 5, of which 3 were waited for; matrix products, arithmetic and copies ran while one was open for 11% of the time, Pallas kernels for 0%

commit v1 on v0

v1 whole, which is shorter than its diff:
```python
import functools

import jax
import jax.numpy as jnp
from jax import lax
from jax.experimental import pallas as pl
from jax.experimental.pallas import tpu as pltpu
from jax.sharding import PartitionSpec as P

F32 = jnp.float32
BF16 = jnp.bfloat16
ANY = pl.BlockSpec(memory_space=pl.ANY)
VMEM = pl.BlockSpec(memory_space=pltpu.VMEM)
SMEM = pl.BlockSpec(memory_space=pltpu.SMEM)


def rotate_kernel(own_ref, *refs):
    *piece_refs, rotation_ref, out_ref = refs
    rows = piece_refs[0].shape[0]
    groups, _, width = out_ref.shape
    for piece, ref in enumerate(piece_refs):
        product = jnp.dot(ref[...], rotation_ref[...], preferred_element_type=F32)
        for q in range(groups):
            out_ref[q ^ own_ref[0], piece * rows : (piece + 1) * rows, :] = product[
                :, q * width : (q + 1) * width
            ].astype(BF16)


def rotate(own, pieces, rotation, groups):
    rows = pieces[0].shape[0]
    width = rotation.shape[1] // groups
    return pl.pallas_call(
        rotate_kernel,
        out_shape=jax.ShapeDtypeStruct((groups, len(pieces) * rows, width), BF16),
        in_specs=[SMEM] + [VMEM] * (len(pieces) + 1),
        out_specs=VMEM,
        cost_estimate=pl.CostEstimate(
            flops=2 * len(pieces) * rows * rotation.size,
            bytes_accessed=2 * (len(pieces) * pieces[0].size + rotation.size),
            transcendentals=0,
        ),
        name="rotate",
    )(own, *pieces, rotation)


def update_kernel(place_ref, codes_ref, values_ref, codebook_ref, out_ref, total_ref):
    tile, width = out_ref.shape
    chunk = values_ref.shape[0]
    step, last = pl.program_id(1), pl.num_programs(1) - 1

    @pl.when(step == 0)
    def _():
        total_ref[...] = jnp.zeros_like(total_ref)

    first = place_ref[1] + pl.program_id(0) * tile
    slot = lax.broadcasted_iota(jnp.int32, (tile, chunk), 0)
    hit = jnp.where(slot == codes_ref[...] - first, 1.0, 0.0).astype(BF16)
    ones = jnp.ones((chunk, width), BF16)
    total_ref[...] += jnp.dot(
        hit, jnp.concatenate([values_ref[...], ones], axis=1), preferred_element_type=F32
    )

    @pl.when(step == last)
    def _():
        out_ref[...] = (
            (total_ref[:, :width] + codebook_ref[0].astype(F32)) / (total_ref[:, width:] + 1.0)
        ).astype(BF16)


def update(place, codes, values, codebook, owned):
    rows, width = values.shape
    chunk, tile = min(rows, 4096), min(owned, 256)
    per = owned // tile
    return pl.pallas_call(
        update_kernel,
        out_shape=jax.ShapeDtypeStruct((owned, width), BF16),
        grid_spec=pltpu.PrefetchScalarGridSpec(
            num_scalar_prefetch=1,
            grid=(per, rows // chunk),
            in_specs=[
                pl.BlockSpec((1, chunk), lambda k, r, place: (0, r)),
                pl.BlockSpec((chunk, width), lambda k, r, place: (r, 0)),
                pl.BlockSpec((1, tile, width), lambda k, r, place: (place[0], place[2] * per + k, 0)),
            ],
            out_specs=pl.BlockSpec((tile, width), lambda k, r, place: (k, 0)),
            scratch_shapes=[pltpu.VMEM((tile, 2 * width), F32)],
        ),
        cost_estimate=pl.CostEstimate(
            flops=4 * owned * rows * width, bytes_accessed=2 * rows * width, transcendentals=0
        ),
        name="update",
    )(place, codes, values, codebook)


def stage_kernel(split, place_ref, codes_ref, values_ref, *refs):
    pieces, blocks, (outs, scratch) = refs[: split[0]], refs[split[0] : split[0] + split[1]], (
        refs[split[0] + split[1] + split[2] :][:3],
        refs[split[0] + split[1] + split[2] + 3 :],
    )
    centroid_ref, cross_ref, distance_ref = outs
    table, picked, product, block_sems, cross_sem = scratch
    group, half, own = place_ref[0], place_ref[1], place_ref[2]
    owned, width = blocks[0].shape
    parts, rows = pieces[0].shape[0], pieces[0].shape[2]
    chunk = len(pieces) * rows
    copies = []
    for j, block in enumerate(blocks):
        first = lax.rem(half + j, len(blocks)) * owned
        copies.append(
            pltpu.make_async_copy(
                block,
                centroid_ref.at[group, pl.ds(pl.multiple_of(first, owned), owned), :],
                block_sems.at[j],
            )
        )
        copies[-1].start()
        table[j * owned : (j + 1) * owned, :] = block[...].astype(F32)
    product[...] = jnp.zeros_like(product)
    unroll = 32

    def part(p, _):
        def pick(i, _):
            base = pl.multiple_of(i * unroll, unroll)
            for u in range(unroll):
                code = codes_ref[p * chunk + base + u]
                picked[pl.ds(base + u, 1), :] = table[pl.ds(code, 1), :]
            return 0

        lax.fori_loop(0, chunk // unroll, pick, 0)
        left = jnp.concatenate([piece[p] for piece in pieces], axis=1)
        product[...] += jnp.dot(left, picked[...].astype(BF16), preferred_element_type=F32)

        @pl.when(p == own)
        def _():
            gap = values_ref[0].astype(F32) - picked[...]
            distance_ref[...] = jnp.sum(gap * gap, axis=1, keepdims=True)

        return 0

    lax.fori_loop(0, parts, part, 0)
    out = pltpu.make_async_copy(
        product, cross_ref.at[:, pl.ds(pl.multiple_of(group * width, width), width)], cross_sem
    )
    out.start()
    out.wait()
    for copy in copies:
        copy.wait()


def stage(place, codes, values, pieces, blocks, carried, shapes):
    groups, count, width = shapes
    owned = blocks[0].shape[0]
    depth, rows = pieces[0].shape[1:]
    chunk = len(pieces) * rows
    fixed = 3 + len(pieces) + len(blocks)
    return pl.pallas_call(
        functools.partial(stage_kernel, (len(pieces), len(blocks), len(carried))),
        out_shape=(
            jax.ShapeDtypeStruct((groups, count, width), BF16),
            jax.ShapeDtypeStruct((depth, groups * width), F32),
            jax.ShapeDtypeStruct((chunk, 1), F32),
        ),
        in_specs=[SMEM, SMEM, pl.BlockSpec((1, chunk, width), lambda: (0, 0, 0))]
        + [VMEM] * (len(pieces) + len(blocks))
        + [ANY] * len(carried),
        out_specs=(ANY, ANY, VMEM),
        scratch_shapes=[
            pltpu.VMEM((count, width), F32),
            pltpu.VMEM((chunk, width), F32),
            pltpu.VMEM((depth, width), F32),
            pltpu.SemaphoreType.DMA((len(blocks),)),
            pltpu.SemaphoreType.DMA,
        ],
        input_output_aliases={fixed + j: j for j in range(len(carried))},
        cost_estimate=pl.CostEstimate(
            flops=2 * depth * width * codes.size * 32,
            bytes_accessed=4 * codes.size * width,
            transcendentals=0,
        ),
        name="stage",
    )(place, codes, values, *pieces, *blocks, *carried)


def hop(value, axis, pairs, name):
    with jax.named_scope(name):
        return lax.ppermute(value, axis, pairs)


def spread(own, size, axis, name):
    have = {0: own}
    bit = size // 2
    while bit:
        pairs = [(i, i ^ bit) for i in range(size)]
        for offset in sorted(have):
            have[offset ^ bit] = hop(have[offset], axis, pairs, f"{name}{offset ^ bit}")
        bit //= 2
    return [have[o] for o in range(size)]


def per_device(n_dp, n_sub, vectors, rotation, codebook, codes):
    groups, count, width = codebook.shape
    rows, depth = vectors.shape
    halves = n_dp // groups
    owned = count // halves
    paired = halves == 2
    ring = list(range(0, n_dp, 2)) + list(range(n_dp - 1, 0, -2)) if paired else list(range(n_dp))
    at = [ring.index(d) for d in range(n_dp)]
    d, sub = lax.axis_index("dp"), lax.axis_index("sub")
    position = jnp.array(at, jnp.int32)[d]
    group, half = position // halves, position % halves

    pieces = spread(vectors, n_sub, "sub", "rows")
    order = jnp.arange(n_sub, dtype=jnp.int32) ^ sub
    mine = codes.reshape(n_sub, rows, groups)[order].reshape(n_sub * rows, groups).T
    labels = lax.all_to_all(
        jnp.broadcast_to(mine[None], (n_dp,) + mine.shape), "dp", 0, 0, tiled=True
    )
    flipped = vectors.T.reshape(n_dp, depth // n_dp, rows)
    turned = lax.all_to_all(flipped, "dp", 0, 0, tiled=True)

    values = rotate(group.reshape(1), pieces, rotation, groups)
    sides = spread(turned, n_sub, "sub", "side")

    parts = [values[0]]
    for t in range(1, groups):
        pairs = [(ring[p], ring[((p // halves) ^ t) * halves + p % halves]) for p in range(n_dp)]
        parts.append(hop(values[t], "dp", pairs, f"swap{t}"))
    whole = [jnp.concatenate(parts, axis=0)]
    bit = 1
    while bit < halves:
        pairs = [(ring[p], ring[(p // halves) * halves + ((p % halves) ^ bit)]) for p in range(n_dp)]
        whole = whole + [hop(w, "dp", pairs, f"join{bit}") for w in whole]
        bit *= 2
    gathered = jnp.concatenate(whole, axis=0)
    source = jnp.array(
        [
            [
                ring[((p // halves) ^ t) * halves + ((p % halves) ^ e)]
                for e in range(halves)
                for t in range(groups)
            ]
            for p in range(n_dp)
        ],
        jnp.int32,
    )[position]
    by_group = labels.transpose(1, 0, 2)
    own_labels = lax.dynamic_index_in_dim(by_group, group, 0, keepdims=False)[source]
    place = jnp.stack([group, half * owned, half]).astype(jnp.int32)
    block = update(place, own_labels.reshape(1, -1), gathered, codebook, owned)

    shapes = codebook.shape
    carried, distances, seen = (), [], []

    def finish(target, turn, blocks, carried):
        label = lax.dynamic_index_in_dim(by_group, target, 0, keepdims=False).reshape(-1)
        label = (label + (count - turn * owned)) % count
        value = lax.dynamic_index_in_dim(values, target ^ group, 0)
        spot = jnp.stack([target, turn, d]).astype(jnp.int32)
        return stage(spot, label, value, sides, blocks, carried, shapes)

    if paired:
        inner = [(ring[p], ring[p ^ 1]) for p in range(n_dp)]
        outer = [(ring[p], ring[(p - 1 if p % 2 == 0 else p + 1) % n_dp]) for p in range(n_dp)]
        a, b = block, block
        for s in range(1, groups + 1):
            if s < groups:
                a_next = hop(b, "dp", inner, f"inner{s}")
                b_next = hop(a, "dp", outer, f"outer{s}")
            else:
                cut = owned // 2
                a_next = jnp.concatenate(
                    [hop(b[:cut], "dp", inner, f"inner{s}"), hop(a[cut:], "dp", outer, f"outer{s}")],
                    axis=0,
                )
                b_next = a_next
            sign = 1 - 2 * half
            if s % 2:
                target, blocks = (group + sign * ((s - 1) // 2)) % groups, [a, a_next]
            else:
                target, blocks = (group - sign * (s // 2)) % groups, [b_next, b]
            a, b = a_next, b_next
            *carried, distance = finish(target, half, blocks, carried)
            distances.append(distance)
            seen.append(target)
    else:
        table = lax.all_gather(block, "dp", axis=0, tiled=True).reshape(groups, count, width)
        for g in range(groups):
            target = jnp.int32(g)
            *carried, distance = finish(target, jnp.int32(0), [table[g]], carried)
            distances.append(distance)
            seen.append(target)
    centroid, cross = carried
    distance = jnp.stack([x.reshape(n_sub, rows) for x in distances])
    slot = jnp.argmax(jnp.stack(seen)[None] == jnp.arange(groups)[:, None], axis=1)
    distance = distance[slot][:, order].reshape(groups, n_sub * rows)
    return centroid, distance.T, cross


def solution(mesh):
    placed = (P(("dp", "sub"), None), P(None, "sub"), P("sub", None, None), P("dp", "sub"))
    return jax.shard_map(
        functools.partial(per_device, mesh.shape["dp"], mesh.shape["sub"]),
        mesh=mesh,
        in_specs=placed,
        out_specs=(P("sub", None, None), P("dp", "sub"), P("dp", "sub")),
        check_vma=False,
    )
```

time: 517 us -> 144 us (0.28)
  waiting for transfers between devices: 415 us -> 31.1 us
  Pallas kernels: 0 us -> 50 us
  other arithmetic: 43.2 us -> 12.4 us
  starting transfers between devices: 3.81 us -> 30.5 us
  local copies, waits for them, and re-layouts: 30.9 us -> 14.6 us
  matrix products: 9.6 us -> 0 us
  between operations: 13.9 us -> 4.85 us
    psum x1 -> x0, waiting for transfers between devices: 271 us -> none  [per_device(): totals, members = lax.psum((totals, members), 'dp')]
    reduce_scatter x1 -> x0, waiting for transfers between devices: 79.6 us -> none  [per_device(): cross = lax.psum_scatter(product, 'dp', scatter_dimension=0, tiled=True)]
    all_gather x2 -> x0, waiting for transfers between devices: 62.6 us -> none  [the longest x1 62.6 us: per_device(): lax.all_gather(rotation, 'sub', axis=1, tiled=True)]
    pallas_call x0 -> x6, Pallas kernels: none -> 50 us  [the longest x4 36.8 us: stage(): pl.pallas_call(functools.partial(stage_kernel, (len(pieces), len(blocks),...]
    ppermute x0 -> x18, waiting for transfers between devices: none -> 26.9 us  [hop(): return lax.ppermute(value, axis, pairs)]
    unnamed x6 -> x0, other arithmetic: 26.6 us -> none
    gather x2 -> x5, local copies, waits for them, and re-layouts: 26 us -> 2.87 us  [the longest x3 1.74 us: per_device(): distance = distance[slot][:, order].reshape(groups, n_sub * rows)]
    ppermute x0 -> x18, starting transfers between devices: none -> 18.8 us  [hop(): return lax.ppermute(value, axis, pairs)]
  transfers between devices with their start and end apart: 5 -> 20, of which waited for: 3 -> 8; matrix products, arithmetic and copies ran while one was open for 11% -> 13% of each run, Pallas kernels for 0% -> 28%
where the time goes in v1:
time: 144 us; the launch traced here: 143 us
  Pallas kernels  50 us (35%)
  waiting for transfers between devices  31.1 us (22%)
  starting transfers between devices  30.5 us (21%)
  local copies, waits for them, and re-layouts  14.6 us (10%)
  other arithmetic  12.4 us (9%)
  between operations  4.85 us (3%)
    pallas_call x4, Pallas kernels, stage(): pl.pallas_call(functools.partial(stage_kernel, (len(pieces), len(blocks),...  36.8 us
    ppermute x18, waiting for transfers between devices, hop(): return lax.ppermute(value, axis, pairs)  26.9 us
    ppermute x18, starting transfers between devices, hop(): return lax.ppermute(value, axis, pairs)  18.8 us
    pallas_call x1, Pallas kernels, update(): pl.pallas_call(update_kernel, out_shape=jax.ShapeDtypeStruct((owned, widt...  8.86 us
    all_to_all x1, starting transfers between devices, per_device(): turned = lax.all_to_all(flipped, 'dp', 0, 0, tiled=True)  5.86 us
    all_to_all x1, starting transfers between devices, per_device(): lax.all_to_all(jnp.broadcast_to(mine[None], (n_dp,) + mine.shape), 'dp',...  5.83 us
    unnamed x32, local copies, waits for them, and re-layouts  5.55 us
    pallas_call x4, other arithmetic, stage(): pl.pallas_call(functools.partial(stage_kernel, (len(pieces), len(blocks),...  4.37 us
  transfers between devices with their start and end apart: 20, of which 8 were waited for; matrix products, arithmetic and copies ran while one was open for 13% of the time, Pallas kernels for 28%

profile of v1, /device:TPU:0, one launch (start us, length us, event | category | flops | bytes accessed | tf_op | source)
XLA Modules:
  0.0 143.3 jit_solution(15833883982715020668)
XLA Ops:
  0.6 3.0 %collective-permute-start.1 = (bf16[128,2048]{1,0:T(8,128)(2,1)}, bf16[128,2048]{1,0:T(8,128)(2,1)S(1)}, u32[]{:S(2)}, u32[]{:S(2)}) collective-permute-start(bf16[128,2048]{1,0:T(8,128)(2,1)} %refs_0_.1), channel_id=1, source_target_pairs={{0,2},{1,3},{2,0},{3,1},{4,6},{5,7},{6,4},{7,5},{8,10},{9,11},{10,... | collective-permute-start | bytes 1572872 | tf_op jit(solution)/shard_map/rows2/ppermute | solution.py:186
  3.7 1.2 dynamic_slice.25
  6.9 0.7 fusion.6
  7.6 0.6 gather_fusion
  8.2 0.6 broadcast_in_dim.4
  8.8 5.8 %all-to-all-start = ((s32[8,4,512]{2,1,0:T(4,128)}), s32[8,4,512]{2,1,0:T(4,128)S(1)}, u32[]{:S(2)}, u32[]{:S(2)}) async-start(s32[8,4,512]{2,1,0:T(4,128)} %broadcast_in_dim.4), calls=%async_computation | async-start | bytes 131072 | tf_op jit(solution)/shard_map/all_to_all | solution.py:215
  16.7 0.7 add_add_fusion.3.place_ref
  17.3 0.1 pad_add_fusion.1
  17.4 0.6 iota_reduce_fusion
  18.0 0.6 add_add_fusion.2.place_ref
  18.6 2.0 %copy.21 = bf16[2048,128]{1,0:T(8,128)(2,1)} copy(bf16[2048,128]{0,1:T(8,128)(2,1)} %bitcast.56) | data formatting | bytes 1048576 | tf_op jit(solution)/shard_map/transpose | solution.py:218
  20.7 0.2 collective-permute-start.2
  20.9 0.7 add_add_fusion.1.place_ref
  21.6 5.9 %all-to-all-start.1 = ((bf16[8,256,128]{2,1,0:T(8,128)(2,1)}), bf16[8,256,128]{2,1,0:T(8,128)(2,1)S(1)}, u32[]{:S(2)}, u32[]{:S(2)}) async-start(bf16[8,256,128]{2,1,0:T(8,128)(2,1)} %bitcast.11), calls=%async_computation.1 | async-start | bytes 1048576 | tf_op jit(solution)/shard_map/all_to_all | solution.py:219
  27.4 0.6 add_add_fusion.place_ref
  28.0 0.7 pad_add_fusion.place_ref
  28.7 0.1 dynamic-slice_add_fusion
  28.8 0.6 gather_fusion.1
  29.4 0.6 copy.24
  30.0 0.8 copy-done.2
  30.8 0.8 copy-done.3
  31.6 4.3 %rotate.1 = bf16[4,512,128]{2,1,0:T(8,128)(2,1)} custom-call(s32[1]{0:T(128)} %bitcast.9.own_ref, bf16[128,2048]{1,0:T(8,128)(2,1)} %refs_0_.1, bf16[128,2048]{1,0:T(8,128)(2,1)} %copy-done.2, bf16[128,2048]{1,0:T(8,128)(2,1)} %copy-done.1, bf16[128,2048]{1,0:T(8,128)(2,1)} %copy-done.3, bf16[2048,512]{1,0:T(8,128)(2,1)} %refs_4_.1), custom_call_target="tpu_custom_call" | custom-call | flops 1073741824 | bytes 4194304 | tf_op jit(solution)/shard_map/rotate/pallas_call | solution.py:32
  35.9 2.1 %constant_dynamic-slice_fusion = (bf16[1,512,128]{2,1,0:T(8,128)(2,1)}, bf16[1,512,128]{2,1,0:T(8,128)(2,1)}, bf16[1,512,128]{2,1,0:T(8,128)(2,1)}, bf16[512,128...) fusion(bf16[4,512,128]{2,1,0:T(8,128)(2,1)} %rotate.1, ...), kind=kLoop, calls=%fused_computation.43 | loop fusion | bytes 2097168 | tf_op jit(solution)/shard_map/jit(dynamic_index_in_dim)/dynamic_slice | solution.py:257
  38.0 2.9 %collective-permute-start.6 = (bf16[512,128]{1,0:T(8,128)(2,1)S(1)}, bf16[512,128]{1,0:T(8,128)(2,1)S(1)}, u32[]{:S(2)}, u32[]{:S(2)}) collective-permute-start(bf16[512,128]{1,0:T(8,128)(2,1)S(1)} %get-tuple-element.34), channel_id=1, source_target_pairs={{0,16},{8,24},{16,0},{24,8},{28,12},{20,4},{12,28},{4,20},{1,17},{... | collective-permute-start | bytes 393224 | tf_op jit(solution)/shard_map/swap1/ppermute | solution.py:186
  40.9 2.4 %collective-permute-start.7 = (bf16[512,128]{1,0:T(8,128)(2,1)S(1)}, bf16[512,128]{1,0:T(8,128)(2,1)S(1)}, u32[]{:S(2)}, u32[]{:S(2)}) collective-permute-start(bf16[512,128]{1,0:T(8,128)(2,1)S(1)} %get-tuple-element.33), channel_id=1, source_target_pairs={{0,28},{8,20},{16,12},{24,4},{28,0},{20,8},{12,16},{4,24},{1,29},{... | collective-permute-start | bytes 393224 | tf_op jit(solution)/shard_map/swap2/ppermute | solution.py:186
  43.3 0.6 add_select_fusion.codes_ref
  43.9 4.1 %all-to-all-done.1.refs_0_ = bf16[8,256,128]{2,1,0:T(8,128)(2,1)S(1)} async-done(((bf16[8,256,128]{2,1,0:T(8,128)(2,1)}), bf16[8,256,128]{2,1,0:T(8,128)(2,1)S(1)}, u32[]{:S(2)}, u32[]{:S(2)}) %all-to-all-start.1) | async-done | bytes 524320 | tf_op jit(solution)/shard_map/all_to_all | solution.py:219
  48.1 0.5 collective-permute-start.4
  48.6 3.2 %collective-permute-done.6 = bf16[512,128]{1,0:T(8,128)(2,1)S(1)} collective-permute-done((bf16[512,128]{1,0:T(8,128)(2,1)S(1)}, bf16[512,128]{1,0:T(8,128)(2,1)S(1)}, u32[]{:S(2)}, u32[]{:S(2)}) %collective-permute-start.6) | collective-permute-done | bytes 131104 | tf_op jit(solution)/shard_map/swap1/ppermute | solution.py:186
  51.8 2.2 %collective-permute-done.8 = bf16[512,128]{1,0:T(8,128)(2,1)S(1)} collective-permute-done((bf16[512,128]{1,0:T(8,128)(2,1)S(1)}, bf16[512,128]{1,0:T(8,128)(2,1)S(1)}, u32[]{:S(2)}, u32[]{:S(2)}) %collective-permute-start.8) | collective-permute-done | bytes 131104 | tf_op jit(solution)/shard_map/swap3/ppermute | solution.py:186
  54.0 1.7 %collective-permute-start.9 = (bf16[2048,128]{1,0:T(8,128)(2,1)S(1)}, bf16[2048,128]{1,0:T(8,128)(2,1)S(1)}, u32[]{:S(2)}, u32[]{:S(2)}) collective-permute-start(bf16[2048,128]{1,0:T(8,128)(2,1)S(1)} %pad_maximum_fusion), channel_id=1, source_target_pairs={{0,8},{8,0},{16,24},{24,16},{28,20},{20,28},{12,4},{4,12},{1,9},{9... | collective-permute-start | bytes 1572872 | tf_op jit(solution)/shard_map/join1/ppermute | solution.py:186
  55.7 0.9 constant_dynamic-update-slice_fusion.4
  56.7 0.5 collective-permute-done.4.refs_2_
  57.2 10.1 %collective-permute-done.9 = bf16[2048,128]{1,0:T(8,128)(2,1)S(1)} collective-permute-done((bf16[2048,128]{1,0:T(8,128)(2,1)S(1)}, bf16[2048,128]{1,0:T(8,128)(2,1)S(1)}, u32[]{:S(2)}, u32[]{:S(2)}) %collective-permute-start.9) | collective-permute-done | bytes 524320 | tf_op jit(solution)/shard_map/join1/ppermute | solution.py:186
  67.4 1.0 copy-done.7
  68.3 8.9 %update.1.refs_4_ = bf16[2048,128]{1,0:T(8,128)(2,1)} custom-call(s32[3]{0:T(128)} %pad_add_fusion.place_ref, s32[1,4096]{1,0:T(1,128)} %bitcast.63, bf16[4096,128]{1,0:T(8,128)(2,1)} %copy-done.7, bf16[4,4096,128]{2,1,0:T(8,128)(2,1)} %codebook_ref.1), custom_call_target="tpu_custom_call" | custom-call | flops 4294967296 | bytes 1048576 | tf_op jit(solution)/shard_map/update/pallas_call | solution.py:74
  77.2 1.8 %collective-permute-start.14 = (bf16[2048,128]{1,0:T(8,128)(2,1)}, bf16[2048,128]{1,0:T(8,128)(2,1)}, u32[]{:S(2)}, u32[]{:S(2)}) collective-permute-start(bf16[2048,128]{1,0:T(8,128)(2,1)} %update.1.refs_4_), channel_id=1, source_target_pairs={{0,8},{8,0},{16,24},{24,16},{28,20},{20,28},{12,4},{4,12},{1,9},{9... | collective-permute-start | bytes 1572872 | tf_op jit(solution)/shard_map/inner1/ppermute | solution.py:186
  79.0 0.3 collective-permute-start.10
  79.3 0.6 add_select_fusion.1.codes_ref
  79.9 0.6 add_select_fusion.2.codes_ref
  80.5 0.6 add_select_fusion.3.codes_ref
  81.1 8.9 %collective-permute-done.14.refs_5_ = bf16[2048,128]{1,0:T(8,128)(2,1)} collective-permute-done((bf16[2048,128]{1,0:T(8,128)(2,1)}, bf16[2048,128]{1,0:T(8,128)(2,1)}, u32[]{:S(2)}, u32[]{:S(2)}) %collective-permute-start.14) | collective-permute-done | bytes 524320 | tf_op jit(solution)/shard_map/inner1/ppermute | solution.py:186
  90.0 0.8 collective-permute-start.15
  90.8 1.4 collective-permute-done.10.refs_5_
  92.2 2.1 %collective-permute-start.11 = (bf16[2048,128]{1,0:T(8,128)(2,1)S(1)}, bf16[2048,128]{1,0:T(8,128)(2,1)S(1)}, u32[]{:S(2)}, u32[]{:S(2)}) collective-permute-start(bf16[2048,128]{1,0:T(8,128)(2,1)S(1)} %collective-permute-done.10.refs_5_), channel_id=1, source_target_pairs={{0,8},{8,0},{16,24},{24,16},{28,20},{20,28},{12,4},{4,12},{1,9},{9... | collective-permute-start | bytes 1572872 | tf_op jit(solution)/shard_map/inner2/ppermute | solution.py:186
  94.3 0.8 copy-done.9
  95.1 0.2 copy-done.10
  95.3 9.2 %stage.4 = (bf16[4,4096,128]{2,1,0:T(8,128)(2,1)}, f32[256,512]{1,0:T(8,128)}, f32[512,1]{1,0:T(8,128)}) custom-call(s32[3]{0:T(128)} %add_add_fusion.3.place_ref, s32[4096]{0:T(1024)} %add_select_fusion.codes_ref, bf16[1,512,128]{2,1,0:T(8,128)(2,1)} %get-tuple-element.29.values_ref, bf16[8,256,128]{2,1,0:T(8,128)(2,1)} %copy-done.4, ...), custom_call_target="tpu_custom_call" | custom-call | flops 8589934592 | bytes 2097152 | tf_op jit(solution)/shard_map/stage/pallas_call | solution.py:156
  104.5 1.1 reduce.18
  105.6 0.1 collective-permute-start.16
  105.7 0.6 collective-permute-start.12
  106.3 9.2 %stage.5 = (bf16[4,4096,128]{2,1,0:T(8,128)(2,1)}, f32[256,512]{1,0:T(8,128)}, f32[512,1]{1,0:T(8,128)}) custom-call(s32[3]{0:T(128)} %add_add_fusion.2.place_ref, s32[4096]{0:T(1024)} %add_select_fusion.1.codes_ref, bf16[1,512,128]{2,1,0:T(8,128)(2,1)} %get-tuple-element.30.values_ref, ...), custom_call_target="tpu_custom_call", output_to_operand_aliasing={{0}: (9, {}), {1}: (10, {})} | custom-call | flops 8589934592 | bytes 2097152 | tf_op jit(solution)/shard_map/stage/pallas_call | solution.py:156
  115.6 1.1 reduce.19
  116.7 0.7 collective-permute-done.12.refs_5_
  117.4 2.0 %collective-permute-start.13 = (bf16[1024,128]{1,0:T(8,128)(2,1)S(1)}, bf16[1024,128]{1,0:T(8,128)(2,1)S(1)}, u32[]{:S(2)}, u32[]{:S(2)}) collective-permute-start(bf16[1024,128]{1,0:T(8,128)(2,1)S(1)} %slice.36), channel_id=1, source_target_pairs={{0,8},{8,0},{16,24},{24,16},{28,20},{20,28},{12,4},{4,12},{1,9},{9... | collective-permute-start | bytes 786440 | tf_op jit(solution)/shard_map/inner4/ppermute | solution.py:186
  119.4 0.4 collective-permute-start.17
  119.7 0.4 copy-done.6
  120.1 9.2 %stage.6 = (bf16[4,4096,128]{2,1,0:T(8,128)(2,1)}, f32[256,512]{1,0:T(8,128)}, f32[512,1]{1,0:T(8,128)}) custom-call(s32[3]{0:T(128)} %add_add_fusion.1.place_ref, s32[4096]{0:T(1024)} %add_select_fusion.2.codes_ref, bf16[1,512,128]{2,1,0:T(8,128)(2,1)} %get-tuple-element.31.values_ref, ...), custom_call_target="tpu_custom_call", output_to_operand_aliasing={{0}: (9, {}), {1}: (10, {})} | custom-call | flops 8589934592 | bytes 2097152 | tf_op jit(solution)/shard_map/stage/pallas_call | solution.py:156
  129.3 1.1 reduce.20
  130.5 0.8 pad_maximum_fusion.1.refs_4_
  131.3 9.2 %stage.7 = (bf16[4,4096,128]{2,1,0:T(8,128)(2,1)}, f32[256,512]{1,0:T(8,128)}, f32[512,1]{1,0:T(8,128)}) custom-call(s32[3]{0:T(128)} %add_add_fusion.place_ref, s32[4096]{0:T(1024)} %add_select_fusion.3.codes_ref, bf16[1,512,128]{2,1,0:T(8,128)(2,1)} %get-tuple-element.36.values_ref, ...), custom_call_target="tpu_custom_call", output_to_operand_aliasing={{0}: (9, {}), {1}: (10, {})} | custom-call | flops 8589934592 | bytes 2097152 | tf_op jit(solution)/shard_map/stage/pallas_call | solution.py:156
  140.5 1.1 reduce.21
  141.6 0.6 gather_fusion.2
  142.2 1.2 gather_fusion.3
  (50 shorter events, 0.3 us)
Async XLA Ops:
  0.6 7.0 %copy-start = (s32[512,4]{0,1:T(4,128)S(1)}, s32[512,4]{0,1:T(4,128)}, u32[]{:S(2)}) copy-start(s32[512,4]{0,1:T(4,128)} %param.9) | copy-start | bytes 24580
  0.6 20.0 %collective-permute-start.1 = (bf16[128,2048]{1,0:T(8,128)(2,1)}, bf16[128,2048]{1,0:T(8,128)(2,1)S(1)}, u32[]{:S(2)}, u32[]{:S(2)}) collective-permute-start(bf16[128,2048]{1,0:T(8,128)(2,1)} %refs_0_.1), channel_id=1, source_target_pairs={{0,2},{1,3},{2,0},{3,1},{4,6},{5,7},{6,4},{7,5},{8,10},{9,11},{10,... | collective-permute-start | bytes 1572872 | tf_op jit(solution)/shard_map/rows2/ppermute | solution.py:186
  3.7 26.3 %collective-permute-start = (bf16[128,2048]{1,0:T(8,128)(2,1)}, bf16[128,2048]{1,0:T(8,128)(2,1)S(1)}, u32[]{:S(2)}, u32[]{:S(2)}) collective-permute-start(bf16[128,2048]{1,0:T(8,128)(2,1)} %refs_0_.1), channel_id=1, source_target_pairs={{0,1},{1,0},{2,3},{3,2},{4,5},{5,4},{6,7},{7,6},{8,9},{9,8},{10,11... | collective-permute-start | bytes 1572872 | tf_op jit(solution)/shard_map/rows1/ppermute | solution.py:186
  8.8 12.8 %all-to-all-start = ((s32[8,4,512]{2,1,0:T(4,128)}), s32[8,4,512]{2,1,0:T(4,128)S(1)}, u32[]{:S(2)}, u32[]{:S(2)}) async-start(s32[8,4,512]{2,1,0:T(4,128)} %broadcast_in_dim.4), calls=%async_computation | async-start | bytes 131072 | tf_op jit(solution)/shard_map/all_to_all | solution.py:215
  20.7 9.3 %copy-start.1 = (bf16[128,2048]{1,0:T(8,128)(2,1)}, bf16[128,2048]{1,0:T(8,128)(2,1)S(1)}, u32[]{:S(2)}) copy-start(bf16[128,2048]{1,0:T(8,128)(2,1)S(1)} %collective-permute-done.1.refs_2_) | copy-start | bytes 1572868
  20.7 9.3 %collective-permute-start.2 = (bf16[128,2048]{1,0:T(8,128)(2,1)S(1)}, bf16[128,2048]{1,0:T(8,128)(2,1)S(1)}, u32[]{:S(2)}, u32[]{:S(2)}) collective-permute-start(bf16[128,2048]{1,0:T(8,128)(2,1)S(1)} %collective-permute-done.1.refs_2_), channel_id=1, source_target_pairs={{0,1},{1,0},{2,3},{3,2},{4,5},{5,4},{6,7},{7,6},{8,9},{9,8},{10,11... | collective-permute-start | bytes 1572872 | tf_op jit(solution)/shard_map/rows3/ppermute | solution.py:186
  21.6 26.5 %all-to-all-start.1 = ((bf16[8,256,128]{2,1,0:T(8,128)(2,1)}), bf16[8,256,128]{2,1,0:T(8,128)(2,1)S(1)}, u32[]{:S(2)}, u32[]{:S(2)}) async-start(bf16[8,256,128]{2,1,0:T(8,128)(2,1)} %bitcast.11), calls=%async_computation.1 | async-start | bytes 1048576 | tf_op jit(solution)/shard_map/all_to_all | solution.py:219
  30.0 0.8 copy-start.2
  30.8 0.8 copy-start.3
  38.0 13.8 %collective-permute-start.6 = (bf16[512,128]{1,0:T(8,128)(2,1)S(1)}, bf16[512,128]{1,0:T(8,128)(2,1)S(1)}, u32[]{:S(2)}, u32[]{:S(2)}) collective-permute-start(bf16[512,128]{1,0:T(8,128)(2,1)S(1)} %get-tuple-element.34), channel_id=1, source_target_pairs={{0,16},{8,24},{16,0},{24,8},{28,12},{20,4},{12,28},{4,20},{1,17},{... | collective-permute-start | bytes 393224 | tf_op jit(solution)/shard_map/swap1/ppermute | solution.py:186
  40.9 10.9 %collective-permute-start.7 = (bf16[512,128]{1,0:T(8,128)(2,1)S(1)}, bf16[512,128]{1,0:T(8,128)(2,1)S(1)}, u32[]{:S(2)}, u32[]{:S(2)}) collective-permute-start(bf16[512,128]{1,0:T(8,128)(2,1)S(1)} %get-tuple-element.33), channel_id=1, source_target_pairs={{0,28},{8,20},{16,12},{24,4},{28,0},{20,8},{12,16},{4,24},{1,29},{... | collective-permute-start | bytes 393224 | tf_op jit(solution)/shard_map/swap2/ppermute | solution.py:186
  43.3 10.7 %collective-permute-start.8 = (bf16[512,128]{1,0:T(8,128)(2,1)S(1)}, bf16[512,128]{1,0:T(8,128)(2,1)S(1)}, u32[]{:S(2)}, u32[]{:S(2)}) collective-permute-start(bf16[512,128]{1,0:T(8,128)(2,1)S(1)} %get-tuple-element.32), channel_id=1, source_target_pairs={{0,12},{8,4},{16,28},{24,20},{28,16},{20,24},{12,0},{4,8},{1,13},{... | collective-permute-start | bytes 393224 | tf_op jit(solution)/shard_map/swap3/ppermute | solution.py:186
  48.1 29.2 %copy-start.4 = (bf16[8,256,128]{2,1,0:T(8,128)(2,1)}, bf16[8,256,128]{2,1,0:T(8,128)(2,1)S(1)}, u32[]{:S(2)}) copy-start(bf16[8,256,128]{2,1,0:T(8,128)(2,1)S(1)} %all-to-all-done.1.refs_0_) | copy-start | bytes 1572868
  48.1 9.2 %collective-permute-start.4 = (bf16[8,256,128]{2,1,0:T(8,128)(2,1)S(1)}, bf16[8,256,128]{2,1,0:T(8,128)(2,1)S(1)}, u32[]{:S(2)}, u32[]{:S(2)}) collective-permute-start(bf16[8,256,128]{2,1,0:T(8,128)(2,1)S(1)} %all-to-all-done.1.refs_0_), channel_id=1, source_target_pairs={{0,2},{1,3},{2,0},{3,1},{4,6},{5,7},{6,4},{7,5},{8,10},{9,11},{10,... | collective-permute-start | bytes 1572872 | tf_op jit(solution)/shard_map/side2/ppermute | solution.py:186
  48.6 45.7 %collective-permute-start.3 = (bf16[8,256,128]{2,1,0:T(8,128)(2,1)S(1)}, bf16[8,256,128]{2,1,0:T(8,128)(2,1)S(1)}, u32[]{:S(2)}, u32[]{:S(2)}) collective-permute-start(bf16[8,256,128]{2,1,0:T(8,128)(2,1)S(1)} %all-to-all-done.1.refs_0_), channel_id=1, source_target_pairs={{0,1},{1,0},{2,3},{3,2},{4,5},{5,4},{6,7},{7,6},{8,9},{9,8},{10,11... | collective-permute-start | bytes 1572872 | tf_op jit(solution)/shard_map/side1/ppermute | solution.py:186
  54.0 13.3 %collective-permute-start.9 = (bf16[2048,128]{1,0:T(8,128)(2,1)S(1)}, bf16[2048,128]{1,0:T(8,128)(2,1)S(1)}, u32[]{:S(2)}, u32[]{:S(2)}) collective-permute-start(bf16[2048,128]{1,0:T(8,128)(2,1)S(1)} %pad_maximum_fusion), channel_id=1, source_target_pairs={{0,8},{8,0},{16,24},{24,16},{28,20},{20,28},{12,4},{4,12},{1,9},{9... | collective-permute-start | bytes 1572872 | tf_op jit(solution)/shard_map/join1/ppermute | solution.py:186
  57.2 20.0 %copy-start.8 = (bf16[8,256,128]{2,1,0:T(8,128)(2,1)}, bf16[8,256,128]{2,1,0:T(8,128)(2,1)S(1)}, u32[]{:S(2)}) copy-start(bf16[8,256,128]{2,1,0:T(8,128)(2,1)S(1)} %collective-permute-done.4.refs_2_) | copy-start | bytes 1572868
  57.2 37.1 %collective-permute-start.5 = (bf16[8,256,128]{2,1,0:T(8,128)(2,1)S(1)}, bf16[8,256,128]{2,1,0:T(8,128)(2,1)S(1)}, u32[]{:S(2)}, u32[]{:S(2)}) collective-permute-start(bf16[8,256,128]{2,1,0:T(8,128)(2,1)S(1)} %collective-permute-done.4.refs_2_), channel_id=1, source_target_pairs={{0,1},{1,0},{2,3},{3,2},{4,5},{5,4},{6,7},{7,6},{8,9},{9,8},{10,11... | collective-permute-start | bytes 1572872 | tf_op jit(solution)/shard_map/side3/ppermute | solution.py:186
  67.4 1.0 copy-start.7
  77.2 12.8 %collective-permute-start.14 = (bf16[2048,128]{1,0:T(8,128)(2,1)}, bf16[2048,128]{1,0:T(8,128)(2,1)}, u32[]{:S(2)}, u32[]{:S(2)}) collective-permute-start(bf16[2048,128]{1,0:T(8,128)(2,1)} %update.1.refs_4_), channel_id=1, source_target_pairs={{0,8},{8,0},{16,24},{24,16},{28,20},{20,28},{12,4},{4,12},{1,9},{9... | collective-permute-start | bytes 1572872 | tf_op jit(solution)/shard_map/inner1/ppermute | solution.py:186
  79.0 13.2 %collective-permute-start.10 = (bf16[2048,128]{1,0:T(8,128)(2,1)}, bf16[2048,128]{1,0:T(8,128)(2,1)S(1)}, u32[]{:S(2)}, u32[]{:S(2)}) collective-permute-start(bf16[2048,128]{1,0:T(8,128)(2,1)} %update.1.refs_4_), channel_id=1, source_target_pairs={{0,4},{8,16},{16,8},{24,28},{28,24},{20,12},{12,20},{4,0},{1,5},{9... | collective-permute-start | bytes 1572872 | tf_op jit(solution)/shard_map/outer1/ppermute | solution.py:186
  90.0 15.6 %collective-permute-start.15 = (bf16[2048,128]{1,0:T(8,128)(2,1)}, bf16[2048,128]{1,0:T(8,128)(2,1)}, u32[]{:S(2)}, u32[]{:S(2)}) collective-permute-start(bf16[2048,128]{1,0:T(8,128)(2,1)} %collective-permute-done.14.refs_5_), channel_id=1, source_target_pairs={{0,4},{8,16},{16,8},{24,28},{28,24},{20,12},{12,20},{4,0},{1,5},{9... | collective-permute-start | bytes 1572872 | tf_op jit(solution)/shard_map/outer2/ppermute | solution.py:186
  92.2 12.3 %copy-start.12 = (bf16[2048,128]{1,0:T(8,128)(2,1)}, bf16[2048,128]{1,0:T(8,128)(2,1)S(1)}, u32[]{:S(2)}) copy-start(bf16[2048,128]{1,0:T(8,128)(2,1)S(1)} %collective-permute-done.10.refs_5_) | copy-start | bytes 1572868
  92.2 13.6 %collective-permute-start.11 = (bf16[2048,128]{1,0:T(8,128)(2,1)S(1)}, bf16[2048,128]{1,0:T(8,128)(2,1)S(1)}, u32[]{:S(2)}, u32[]{:S(2)}) collective-permute-start(bf16[2048,128]{1,0:T(8,128)(2,1)S(1)} %collective-permute-done.10.refs_5_), channel_id=1, source_target_pairs={{0,8},{8,0},{16,24},{24,16},{28,20},{20,28},{12,4},{4,12},{1,9},{9... | collective-permute-start | bytes 1572872 | tf_op jit(solution)/shard_map/inner2/ppermute | solution.py:186
  94.3 0.8 copy-start.9
  94.3 1.0 copy-start.10
  105.6 13.7 %collective-permute-start.16 = (bf16[2048,128]{1,0:T(8,128)(2,1)}, bf16[2048,128]{1,0:T(8,128)(2,1)S(1)}, u32[]{:S(2)}, u32[]{:S(2)}) collective-permute-start(bf16[2048,128]{1,0:T(8,128)(2,1)} %collective-permute-done.15.refs_4_), channel_id=1, source_target_pairs={{0,8},{8,0},{16,24},{24,16},{28,20},{20,28},{12,4},{4,12},{1,9},{9... | collective-permute-start | bytes 1572872 | tf_op jit(solution)/shard_map/inner3/ppermute | solution.py:186
  105.7 9.8 %copy-start.11 = (bf16[2048,128]{1,0:T(8,128)(2,1)}, bf16[2048,128]{1,0:T(8,128)(2,1)S(1)}, u32[]{:S(2)}) copy-start(bf16[2048,128]{1,0:T(8,128)(2,1)S(1)} %collective-permute-done.11.refs_4_) | copy-start | bytes 1572868
  105.7 11.6 %collective-permute-start.12 = (bf16[2048,128]{1,0:T(8,128)(2,1)S(1)}, bf16[2048,128]{1,0:T(8,128)(2,1)S(1)}, u32[]{:S(2)}, u32[]{:S(2)}) collective-permute-start(bf16[2048,128]{1,0:T(8,128)(2,1)S(1)} %collective-permute-done.11.refs_4_), channel_id=1, source_target_pairs={{0,4},{8,16},{16,8},{24,28},{28,24},{20,12},{12,20},{4,0},{1,5},{9... | collective-permute-start | bytes 1572872 | tf_op jit(solution)/shard_map/outer3/ppermute | solution.py:186
  117.3 12.0 %copy-start.5 = (bf16[2048,128]{1,0:T(8,128)(2,1)}, bf16[2048,128]{1,0:T(8,128)(2,1)S(1)}, u32[]{:S(2)}) copy-start(bf16[2048,128]{1,0:T(8,128)(2,1)S(1)} %collective-permute-done.12.refs_5_) | copy-start | bytes 1572868
  117.4 13.1 %collective-permute-start.13 = (bf16[1024,128]{1,0:T(8,128)(2,1)S(1)}, bf16[1024,128]{1,0:T(8,128)(2,1)S(1)}, u32[]{:S(2)}, u32[]{:S(2)}) collective-permute-start(bf16[1024,128]{1,0:T(8,128)(2,1)S(1)} %slice.36), channel_id=1, source_target_pairs={{0,8},{8,0},{16,24},{24,16},{28,20},{20,28},{12,4},{4,12},{1,9},{9... | collective-permute-start | bytes 786440 | tf_op jit(solution)/shard_map/inner4/ppermute | solution.py:186
  119.3 0.8 copy-start.6
  119.4 11.1 %collective-permute-start.17 = (bf16[1024,128]{1,0:T(8,128)(2,1)S(1)}, bf16[1024,128]{1,0:T(8,128)(2,1)S(1)}, u32[]{:S(2)}, u32[]{:S(2)}) collective-permute-start(bf16[1024,128]{1,0:T(8,128)(2,1)S(1)} %slice.37), channel_id=1, source_target_pairs={{0,4},{8,16},{16,8},{24,28},{28,24},{20,12},{12,20},{4,0},{1,5},{9... | collective-permute-start | bytes 786440 | tf_op jit(solution)/shard_map/outer4/ppermute | solution.py:186
